TPU v7x, 32 devices: a whole 2x2x4 slice. The times are simulated.
32 devices in a mesh: pair: 8 (over z, y), aux: 4 (over x, core).
Axes of the slice: x: 2, y: 2, z: 4, core: 2. Of those that a mesh axis runs over, the one named last changes fastest.
Arguments:
- pair_factors: bfloat16 [16384, 16384], P('pair', 'aux'), may hold values from -0.077339804 to 0.077339804
- pair_weights: float32 [16384], P('pair'), may hold values from 0.08 to 0.8
- probes: float32 [16384, 64], P('aux'), may hold values from -12 to 12
Outputs:
- last_vectors: float32 [16384, 64], P('aux', 'pair')
- moments: float32 [9], replicated
- energy: float32 [1], replicated
All inputs are finite; a program needn't handle non-finite values.
Results may differ from a plain program's by a relative error of at most 0.019.
Values may be sent and summed in bfloat16 or wider, within the bound.
No kernel may reach another device: no remote copies, remote signals or barrier semaphores. Data moves between devices by JAX's collectives and lax.ppermute only.
A program may use at most 64 MiB of HBM per device.

v0:
```python
import jax
import jax.numpy as jnp
import numpy as np
from jax import lax
from jax.sharding import PartitionSpec as P

ITERS = 8
spread = 5.0


def cheb_coefficients(order_count):
    node_count = 64
    angles = (np.arange(node_count) + 0.5) * np.pi / node_count
    samples = np.log(1.0 + spread * (np.cos(angles) + 1.0) / 2.0)
    values = [
        2.0 / node_count * np.sum(samples * np.cos(degree * angles))
        for degree in range(order_count)
    ]
    values[0] = values[0] / 2.0
    return np.array(values)


def per_device(pair_factors, pair_weights, probes):
    probe_total = probes.shape[1]
    divisor = probe_total * probes.shape[0] * lax.axis_size("aux")
    share = probe_total // lax.axis_size("pair")
    start = lax.axis_index("pair") * share
    own_probes = lax.dynamic_slice_in_dim(probes, start, share, 1)
    partials = [jnp.sum(own_probes * own_probes)]
    previous = probes
    current = probes
    for degree in range(ITERS):
        rows = jnp.dot(
            pair_factors, current.astype(jnp.bfloat16), preferred_element_type=jnp.float32
        )
        rows = lax.psum(rows, "aux")
        scaled = (pair_weights[:, None] * rows).astype(jnp.bfloat16)
        image = lax.psum(
            lax.dot_general(
                pair_factors, scaled, (((0,), (0,)), ((), ())), preferred_element_type=jnp.float32
            ),
            "pair",
        )
        mapped = 2.0 / spread * image - current
        following = mapped if degree == 0 else 2.0 * mapped - previous
        previous, current = (current, following)
        own_share = lax.dynamic_slice_in_dim(current, start, share, 1)
        partials.append(jnp.sum(own_probes * own_share))
    own_share = lax.dynamic_slice_in_dim(current, start, share, 1)
    totals = lax.psum(jnp.stack(partials), ("pair", "aux"))
    moments = totals / divisor
    coefficients = jnp.asarray(cheb_coefficients(ITERS + 1)).astype(moments.dtype)
    energy = jnp.sum(coefficients * moments).reshape(1)
    return (own_share, moments, energy)


def solution(mesh):
    placed = (P("pair", "aux"), P("pair"), P("aux", None))
    return jax.shard_map(
        per_device,
        mesh=mesh,
        in_specs=placed,
        out_specs=(P("aux", "pair"), P(), P()),
        check_vma=False,
    )
```

profile of v0, /device:TPU:0, one launch (start us, length us, event | category | flops | bytes accessed | tf_op | source)
XLA Modules:
  0.0 1159.6 jit_solution(14180925838934480082)
XLA Ops:
  7.2 11.6 fusion.7
  18.8 39.1 %all-reduce.17.cloned.1.call-done = f32[2048,64]{1,0:T(8,128)} async-done(((f32[2048,64]{1,0:T(8,128)}), f32[2048,64]{1,0:T(8,128)}) %all-reduce.17.cloned.1.call-update) | async-done | bytes 524304 | tf_op jit(solution)/shard_map/psum | solution.py:36
  58.0 10.3 convolution_bitcast_fusion.7
  68.3 78.9 %all-reduce.19.cloned.1.call-done = f32[4096,64]{0,1:T(8,128)} async-done(((f32[4096,64]{0,1:T(8,128)}), f32[4096,64]{0,1:T(8,128)}) %all-reduce.19.cloned.1.call-update) | async-done | bytes 1048592 | tf_op jit(solution)/shard_map/psum | solution.py:38
  148.6 9.2 convolution_bitcast_fusion.14
  158.4 35.5 %all-reduce.21.cloned.1.call-done = f32[2048,64]{1,0:T(8,128)} async-done(((f32[2048,64]{1,0:T(8,128)}), f32[2048,64]{1,0:T(8,128)}) %all-reduce.21.cloned.1.call-update) | async-done | bytes 524304 | tf_op jit(solution)/shard_map/psum | solution.py:36
  193.8 10.3 convolution_bitcast_fusion.6
  204.2 79.0 %all-reduce.23.cloned.1.call-done = f32[4096,64]{0,1:T(8,128)} async-done(((f32[4096,64]{0,1:T(8,128)}), f32[4096,64]{0,1:T(8,128)}) %all-reduce.23.cloned.1.call-update) | async-done | bytes 1048592 | tf_op jit(solution)/shard_map/psum | solution.py:38
  284.6 9.2 convolution_bitcast_fusion.13
  293.8 36.0 %all-reduce.25.cloned.1.call-done = f32[2048,64]{1,0:T(8,128)} async-done(((f32[2048,64]{1,0:T(8,128)}), f32[2048,64]{1,0:T(8,128)}) %all-reduce.25.cloned.1.call-update) | async-done | bytes 524304 | tf_op jit(solution)/shard_map/psum | solution.py:36
  329.8 10.3 convolution_bitcast_fusion.5
  340.2 79.0 %all-reduce.27.cloned.1.call-done = f32[4096,64]{0,1:T(8,128)} async-done(((f32[4096,64]{0,1:T(8,128)}), f32[4096,64]{0,1:T(8,128)}) %all-reduce.27.cloned.1.call-update) | async-done | bytes 1048592 | tf_op jit(solution)/shard_map/psum | solution.py:38
  420.6 9.2 convolution_bitcast_fusion.12
  430.0 35.8 %all-reduce.29.cloned.1.call-done = f32[2048,64]{1,0:T(8,128)} async-done(((f32[2048,64]{1,0:T(8,128)}), f32[2048,64]{1,0:T(8,128)}) %all-reduce.29.cloned.1.call-update) | async-done | bytes 524304 | tf_op jit(solution)/shard_map/psum | solution.py:36
  465.8 10.3 convolution_bitcast_fusion.4
  476.2 79.0 %all-reduce.31.cloned.1.call-done = f32[4096,64]{0,1:T(8,128)} async-done(((f32[4096,64]{0,1:T(8,128)}), f32[4096,64]{0,1:T(8,128)}) %all-reduce.31.cloned.1.call-update) | async-done | bytes 1048592 | tf_op jit(solution)/shard_map/psum | solution.py:38
  557.5 9.1 convolution_bitcast_fusion.11
  566.7 36.0 %all-reduce.33.cloned.1.call-done = f32[2048,64]{1,0:T(8,128)} async-done(((f32[2048,64]{1,0:T(8,128)}), f32[2048,64]{1,0:T(8,128)}) %all-reduce.33.cloned.1.call-update) | async-done | bytes 524304 | tf_op jit(solution)/shard_map/psum | solution.py:36
  602.7 10.2 convolution_bitcast_fusion.3
  613.0 78.9 %all-reduce.35.cloned.1.call-done = f32[4096,64]{0,1:T(8,128)} async-done(((f32[4096,64]{0,1:T(8,128)}), f32[4096,64]{0,1:T(8,128)}) %all-reduce.35.cloned.1.call-update) | async-done | bytes 1048592 | tf_op jit(solution)/shard_map/psum | solution.py:38
  694.7 9.1 convolution_bitcast_fusion.10
  704.0 35.8 %all-reduce.37.cloned.1.call-done = f32[2048,64]{1,0:T(8,128)} async-done(((f32[2048,64]{1,0:T(8,128)}), f32[2048,64]{1,0:T(8,128)}) %all-reduce.37.cloned.1.call-update) | async-done | bytes 524304 | tf_op jit(solution)/shard_map/psum | solution.py:36
  739.8 10.2 convolution_bitcast_fusion.2
  750.2 78.8 %all-reduce.39.cloned.1.call-done = f32[4096,64]{0,1:T(8,128)} async-done(((f32[4096,64]{0,1:T(8,128)}), f32[4096,64]{0,1:T(8,128)}) %all-reduce.39.cloned.1.call-update) | async-done | bytes 1048592 | tf_op jit(solution)/shard_map/psum | solution.py:38
  841.2 36.0 %all-reduce.41.cloned.1.call-done = f32[2048,64]{1,0:T(8,128)} async-done(((f32[2048,64]{1,0:T(8,128)}), f32[2048,64]{1,0:T(8,128)}) %all-reduce.41.cloned.1.call-update) | async-done | bytes 524304 | tf_op jit(solution)/shard_map/psum | solution.py:36
  877.2 10.2 convolution_bitcast_fusion.1
  887.5 78.9 %all-reduce.43.cloned.1.call-done = f32[4096,64]{0,1:T(8,128)} async-done(((f32[4096,64]{0,1:T(8,128)}), f32[4096,64]{0,1:T(8,128)}) %all-reduce.43.cloned.1.call-update) | async-done | bytes 1048592 | tf_op jit(solution)/shard_map/psum | solution.py:38
  969.4 9.1 convolution_bitcast_fusion.8
  978.8 35.7 %all-reduce.45.cloned.1.call-done = f32[2048,64]{1,0:T(8,128)} async-done(((f32[2048,64]{1,0:T(8,128)}), f32[2048,64]{1,0:T(8,128)}) %all-reduce.45.cloned.1.call-update) | async-done | bytes 524304 | tf_op jit(solution)/shard_map/psum | solution.py:36
  1014.6 10.3 convolution_bitcast_fusion
  1024.9 78.9 %all-reduce.47.cloned.1.call-done = f32[4096,64]{0,1:T(8,128)} async-done(((f32[4096,64]{0,1:T(8,128)}), f32[4096,64]{0,1:T(8,128)}) %all-reduce.47.cloned.1.call-update) | async-done | bytes 1048592 | tf_op jit(solution)/shard_map/psum | solution.py:38
  1112.1 39.5 %psum.135 = f32[9]{0:T(128)S(1)} all-reduce(f32[9]{0:T(128)S(1)} %stack.39), channel_id=1, replica_groups=mesh['pair'=8,'aux'=4] {'pair','aux'}, use_global_device_ids=true, to_apply=%region_25.0 | all-reduce | flops 9 | bytes 72 | tf_op jit(solution)/shard_map/psum | solution.py:50
  (57 shorter events, 35.9 us)
Async XLA Ops:
  7.2 50.8 %copy-start.5 = (f32[2048]{0:T(1024)S(1)}, f32[2048]{0:T(1024)}, u32[]{:S(2)}) copy-start(f32[2048]{0:T(1024)} %param.5) | copy-start | bytes 24580
  7.2 50.8 %all-reduce.17.cloned.1.call-start = ((), (), s32[]{:S(2)}) async-start(), calls=%async_computation | async-start | bytes 2097152 | tf_op jit(solution)/shard_map/psum | solution.py:36
  18.8 128.5 %copy-start.4 = (f32[4096,64]{0,1:T(8,128)S(1)}, f32[4096,64]{0,1:T(8,128)}, u32[]{:S(2)}) copy-start(f32[4096,64]{0,1:T(8,128)} %param.6) | copy-start | bytes 3145732
  18.8 128.4 %all-reduce.19.cloned.1.call-start = ((), (), s32[]{:S(2)}) async-start(), calls=%async_computation.1 | async-start | bytes 2097152 | tf_op jit(solution)/shard_map/psum | solution.py:38
  68.3 125.5 %all-reduce.21.cloned.1.call-start = ((), (), s32[]{:S(2)}) async-start(), calls=%async_computation.2 | async-start | bytes 2097152 | tf_op jit(solution)/shard_map/psum | solution.py:36
  157.8 125.4 %all-reduce.23.cloned.1.call-start = ((), (), s32[]{:S(2)}) async-start(), calls=%async_computation.3 | async-start | bytes 2097152 | tf_op jit(solution)/shard_map/psum | solution.py:38
  204.1 125.7 %all-reduce.25.cloned.1.call-start = ((), (), s32[]{:S(2)}) async-start(), calls=%async_computation.4 | async-start | bytes 2097152 | tf_op jit(solution)/shard_map/psum | solution.py:36
  293.8 125.4 %all-reduce.27.cloned.1.call-start = ((), (), s32[]{:S(2)}) async-start(), calls=%async_computation.5 | async-start | bytes 2097152 | tf_op jit(solution)/shard_map/psum | solution.py:38
  340.1 125.7 %all-reduce.29.cloned.1.call-start = ((), (), s32[]{:S(2)}) async-start(), calls=%async_computation.6 | async-start | bytes 2097152 | tf_op jit(solution)/shard_map/psum | solution.py:36
  429.8 125.4 %all-reduce.31.cloned.1.call-start = ((), (), s32[]{:S(2)}) async-start(), calls=%async_computation.7 | async-start | bytes 2097152 | tf_op jit(solution)/shard_map/psum | solution.py:38
  476.1 126.6 %all-reduce.33.cloned.1.call-start = ((), (), s32[]{:S(2)}) async-start(), calls=%async_computation.8 | async-start | bytes 2097152 | tf_op jit(solution)/shard_map/psum | solution.py:36
  556.6 1.0 copy-start
  566.7 125.2 %all-reduce.35.cloned.1.call-start = ((), (), s32[]{:S(2)}) async-start(), calls=%async_computation.9 | async-start | bytes 2097152 | tf_op jit(solution)/shard_map/psum | solution.py:38
  613.0 126.8 %all-reduce.37.cloned.1.call-start = ((), (), s32[]{:S(2)}) async-start(), calls=%async_computation.10 | async-start | bytes 2097152 | tf_op jit(solution)/shard_map/psum | solution.py:36
  693.6 1.0 copy-start.1
  703.8 125.2 %all-reduce.39.cloned.1.call-start = ((), (), s32[]{:S(2)}) async-start(), calls=%async_computation.11 | async-start | bytes 2097152 | tf_op jit(solution)/shard_map/psum | solution.py:38
  750.1 127.0 %all-reduce.41.cloned.1.call-start = ((), (), s32[]{:S(2)}) async-start(), calls=%async_computation.12 | async-start | bytes 2097152 | tf_op jit(solution)/shard_map/psum | solution.py:36
  831.0 1.0 copy-start.2
  841.1 125.2 %all-reduce.43.cloned.1.call-start = ((), (), s32[]{:S(2)}) async-start(), calls=%async_computation.13 | async-start | bytes 2097152 | tf_op jit(solution)/shard_map/psum | solution.py:38
  887.4 127.1 %all-reduce.45.cloned.1.call-start = ((), (), s32[]{:S(2)}) async-start(), calls=%async_computation.14 | async-start | bytes 2097152 | tf_op jit(solution)/shard_map/psum | solution.py:36
  968.4 1.0 copy-start.3
  978.5 173.2 %copy-start.6 = (f32[9]{0:T(128)S(1)}, f32[9]{0:T(128)}, u32[]{:S(2)}) copy-start(f32[9]{0:T(128)} %constant.23.clone) | copy-start | bytes 112
  978.5 125.3 %all-reduce.47.cloned.1.call-start = ((), (), s32[]{:S(2)}) async-start(), calls=%async_computation.15 | async-start | bytes 2097152 | tf_op jit(solution)/shard_map/psum | solution.py:38
Sparse Core Ops, SparseCore 0:
  18.9 39.0 all-reduce.16
  68.4 78.7 all-reduce.18
  157.9 35.8 all-reduce.20
  204.3 78.8 all-reduce.22
  293.9 35.8 all-reduce.24
  340.3 78.8 all-reduce.26
  429.9 35.8 all-reduce.28
  476.2 78.8 all-reduce.30
  566.8 35.8 all-reduce.32
  613.1 78.7 all-reduce.34
  703.9 35.8 all-reduce.36
  750.2 78.7 all-reduce.38
  841.2 35.8 all-reduce.40
  887.5 78.7 all-reduce.42
  978.6 35.8 all-reduce.44
  1025.0 78.7 all-reduce.46
where the time goes:
time: 1170 us; the launch traced here: 1160 us
  waiting for transfers between devices  922 us (79%)
  matrix products  158 us (14%)
  blocking collectives  39.5 us (3%)
  other arithmetic  15.1 us (1%)
  between operations  14.3 us (1%)
    psum x8, waiting for transfers between devices, per_device(): lax.psum(lax.dot_general(pair_factors, scaled, (((0,), (0,)), ((), ())),...  631 us
    psum x8, waiting for transfers between devices, per_device(): rows = lax.psum(rows, 'aux')  290 us
    dot_general x8, matrix products, per_device(): lax.dot_general(pair_factors, scaled, (((0,), (0,)), ((), ())), preferred...  82.2 us
    dot_general x8, matrix products, per_device(): jnp.dot(pair_factors, current.astype(jnp.bfloat16), preferred_element_typ...  75.4 us
    psum x1, blocking collectives, per_device(): totals = lax.psum(jnp.stack(partials), ('pair', 'aux'))  39.5 us
  transfers between devices with their start and end apart: 16, of which 16 were waited for; matrix products, arithmetic and copies ran while one was open for 0% of the time, Pallas kernels for 0%

commit v1 on v0

--- a/solution.py
+++ b/solution.py
@@ -35,11 +35,17 @@
         )
         rows = lax.psum(rows, "aux")
         scaled = (pair_weights[:, None] * rows).astype(jnp.bfloat16)
-        image = lax.psum(
-            lax.dot_general(
-                pair_factors, scaled, (((0,), (0,)), ((), ())), preferred_element_type=jnp.float32
+        image = jnp.sum(
+            lax.all_gather(
+                lax.dot_general(
+                    pair_factors,
+                    scaled,
+                    (((0,), (0,)), ((), ())),
+                    preferred_element_type=jnp.float32,
+                ),
+                "pair",
             ),
-            "pair",
+            axis=0,
         )
         mapped = 2.0 / spread * image - current
         following = mapped if degree == 0 else 2.0 * mapped - previous

time: 1170 us -> 1600 us (1.37)
  waiting for transfers between devices: 922 us -> 1280 us
  local copies, waits for them, and re-layouts: 9.66 us -> 75 us
    all_gather x0 -> x8, waiting for transfers between devices: none -> 1000 us  [per_device(): lax.all_gather(lax.dot_general(pair_factors, scaled, (((0,), (0,)), ((),...]
    psum x8 -> x0, waiting for transfers between devices: 631 us -> none  [per_device(): lax.psum(lax.dot_general(pair_factors, scaled, (((0,), (0,)), ((), ())),...]
    unnamed x14 -> x32, local copies, waits for them, and re-layouts: 3.97 us -> 69.3 us
where the time goes in v1:
time: 1600 us; the launch traced here: 1590 us
  waiting for transfers between devices  1280 us (80%)
  matrix products  158 us (10%)
  local copies, waits for them, and re-layouts  75 us (5%)
  blocking collectives  38.3 us (2%)
  other arithmetic  21.1 us (1%)
    all_gather x8, waiting for transfers between devices, per_device(): lax.all_gather(lax.dot_general(pair_factors, scaled, (((0,), (0,)), ((),...  1000 us
    psum x8, waiting for transfers between devices, per_device(): rows = lax.psum(rows, 'aux')  279 us
    dot_general x8, matrix products, per_device(): lax.dot_general(pair_factors, scaled, (((0,), (0,)), ((), ())), preferred...  82.4 us
    dot_general x8, matrix products, per_device(): jnp.dot(pair_factors, current.astype(jnp.bfloat16), preferred_element_typ...  75.6 us
    unnamed x32, local copies, waits for them, and re-layouts  69.3 us
    psum x1, blocking collectives, per_device(): totals = lax.psum(jnp.stack(partials), ('pair', 'aux'))  38.3 us
  transfers between devices with their start and end apart: 16, of which 16 were waited for; matrix products, arithmetic and copies ran while one was open for 0% of the time, Pallas kernels for 0%

profile of v1, /device:TPU:0, one launch (start us, length us, event | category | flops | bytes accessed | tf_op | source)
XLA Modules:
  0.0 1589.3 jit_solution(4025910925350474887)
XLA Ops:
  7.2 11.6 fusion.7
  18.8 39.1 %all-reduce.9.cloned.1.call-done = f32[2048,64]{1,0:T(8,128)} async-done(((f32[2048,64]{1,0:T(8,128)}), f32[2048,64]{1,0:T(8,128)}) %all-reduce.9.cloned.1.call-update) | async-done | bytes 524304 | tf_op jit(solution)/shard_map/psum | solution.py:36
  58.0 10.3 convolution_bitcast_fusion.7
  68.6 124.9 %all-gather.17.cloned.1.call-done = f32[32768,64]{0,1:T(8,128)} async-done(((f32[4096,64]{0,1:T(8,128)}), f32[32768,64]{0,1:T(8,128)}) %all-gather.17.cloned.1.call-update) | async-done | bytes 8388624 | tf_op jit(solution)/shard_map/all_gather | solution.py:39
  203.8 9.2 convolution_bitcast_fusion.14
  213.0 34.6 %all-reduce.11.cloned.1.call-done = f32[2048,64]{1,0:T(8,128)} async-done(((f32[2048,64]{1,0:T(8,128)}), f32[2048,64]{1,0:T(8,128)}) %all-reduce.11.cloned.1.call-update) | async-done | bytes 524304 | tf_op jit(solution)/shard_map/psum | solution.py:36
  247.6 10.3 convolution_bitcast_fusion.6
  258.2 124.8 %all-gather.19.cloned.1.call-done = f32[32768,64]{0,1:T(8,128)} async-done(((f32[4096,64]{0,1:T(8,128)}), f32[32768,64]{0,1:T(8,128)}) %all-gather.19.cloned.1.call-update) | async-done | bytes 8388624 | tf_op jit(solution)/shard_map/all_gather | solution.py:39
  393.4 9.1 convolution_bitcast_fusion.13
  403.0 34.2 %all-reduce.13.cloned.1.call-done = f32[2048,64]{1,0:T(8,128)} async-done(((f32[2048,64]{1,0:T(8,128)}), f32[2048,64]{1,0:T(8,128)}) %all-reduce.13.cloned.1.call-update) | async-done | bytes 524304 | tf_op jit(solution)/shard_map/psum | solution.py:36
  437.2 10.3 convolution_bitcast_fusion.5
  447.6 125.0 %all-gather.21.cloned.1.call-done = f32[32768,64]{0,1:T(8,128)} async-done(((f32[4096,64]{0,1:T(8,128)}), f32[32768,64]{0,1:T(8,128)}) %all-gather.21.cloned.1.call-update) | async-done | bytes 8388624 | tf_op jit(solution)/shard_map/all_gather | solution.py:39
  592.4 34.4 %all-reduce.15.cloned.1.call-done = f32[2048,64]{1,0:T(8,128)} async-done(((f32[2048,64]{1,0:T(8,128)}), f32[2048,64]{1,0:T(8,128)}) %all-reduce.15.cloned.1.call-update) | async-done | bytes 524304 | tf_op jit(solution)/shard_map/psum | solution.py:36
  626.8 10.3 convolution_bitcast_fusion.4
  637.2 125.0 %all-gather.23.cloned.1.call-done = f32[32768,64]{0,1:T(8,128)} async-done(((f32[4096,64]{0,1:T(8,128)}), f32[32768,64]{0,1:T(8,128)}) %all-gather.23.cloned.1.call-update) | async-done | bytes 8388624 | tf_op jit(solution)/shard_map/all_gather | solution.py:39
  773.6 9.2 convolution_bitcast_fusion.11
  783.2 34.2 %all-reduce.17.cloned.1.call-done = f32[2048,64]{1,0:T(8,128)} async-done(((f32[2048,64]{1,0:T(8,128)}), f32[2048,64]{1,0:T(8,128)}) %all-reduce.17.cloned.1.call-update) | async-done | bytes 524304 | tf_op jit(solution)/shard_map/psum | solution.py:36
  817.4 10.2 convolution_bitcast_fusion.3
  827.7 125.0 %all-gather.25.cloned.1.call-done = f32[32768,64]{0,1:T(8,128)} async-done(((f32[4096,64]{0,1:T(8,128)}), f32[32768,64]{0,1:T(8,128)}) %all-gather.25.cloned.1.call-update) | async-done | bytes 8388624 | tf_op jit(solution)/shard_map/all_gather | solution.py:39
  964.2 9.2 convolution_bitcast_fusion.10
  973.6 34.4 %all-reduce.19.cloned.1.call-done = f32[2048,64]{1,0:T(8,128)} async-done(((f32[2048,64]{1,0:T(8,128)}), f32[2048,64]{1,0:T(8,128)}) %all-reduce.19.cloned.1.call-update) | async-done | bytes 524304 | tf_op jit(solution)/shard_map/psum | solution.py:36
  1008.0 10.2 convolution_bitcast_fusion.2
  1018.3 125.0 %all-gather.27.cloned.1.call-done = f32[32768,64]{0,1:T(8,128)} async-done(((f32[4096,64]{0,1:T(8,128)}), f32[32768,64]{0,1:T(8,128)}) %all-gather.27.cloned.1.call-update) | async-done | bytes 8388624 | tf_op jit(solution)/shard_map/all_gather | solution.py:39
  1154.8 9.1 convolution_bitcast_fusion.9
  1164.2 34.4 %all-reduce.21.cloned.1.call-done = f32[2048,64]{1,0:T(8,128)} async-done(((f32[2048,64]{1,0:T(8,128)}), f32[2048,64]{1,0:T(8,128)}) %all-reduce.21.cloned.1.call-update) | async-done | bytes 524304 | tf_op jit(solution)/shard_map/psum | solution.py:36
  1198.5 10.2 convolution_bitcast_fusion.1
  1208.9 125.0 %all-gather.29.cloned.1.call-done = f32[32768,64]{0,1:T(8,128)} async-done(((f32[4096,64]{0,1:T(8,128)}), f32[32768,64]{0,1:T(8,128)}) %all-gather.29.cloned.1.call-update) | async-done | bytes 8388624 | tf_op jit(solution)/shard_map/all_gather | solution.py:39
  1345.3 9.1 convolution_bitcast_fusion.8
  1354.8 34.3 %all-reduce.23.cloned.1.call-done = f32[2048,64]{1,0:T(8,128)} async-done(((f32[2048,64]{1,0:T(8,128)}), f32[2048,64]{1,0:T(8,128)}) %all-reduce.23.cloned.1.call-update) | async-done | bytes 524304 | tf_op jit(solution)/shard_map/psum | solution.py:36
  1389.1 10.3 convolution_bitcast_fusion
  1399.5 125.1 %all-gather.31.cloned.1.call-done = f32[32768,64]{0,1:T(8,128)} async-done(((f32[4096,64]{0,1:T(8,128)}), f32[32768,64]{0,1:T(8,128)}) %all-gather.31.cloned.1.call-update) | async-done | bytes 8388624 | tf_op jit(solution)/shard_map/all_gather | solution.py:39
  1542.9 38.3 %psum.71 = f32[9]{0:T(128)S(1)} all-reduce(f32[9]{0:T(128)S(1)} %stack.39), channel_id=1, replica_groups=mesh['pair'=8,'aux'=4] {'pair','aux'}, use_global_device_ids=true, to_apply=%region_25.0 | all-reduce | flops 9 | bytes 72 | tf_op jit(solution)/shard_map/psum | solution.py:56
  (83 shorter events, 108.2 us)
Async XLA Ops:
  7.2 50.8 %copy-start.10 = (f32[2048]{0:T(1024)S(1)}, f32[2048]{0:T(1024)}, u32[]{:S(2)}) copy-start(f32[2048]{0:T(1024)} %param.5) | copy-start | bytes 24580
  7.2 50.8 %all-reduce.9.cloned.1.call-start = ((), (), s32[]{:S(2)}) async-start(), calls=%async_computation | async-start | bytes 2097152 | tf_op jit(solution)/shard_map/psum | solution.py:36
  18.8 174.6 %all-gather.17.cloned.1.call-start = ((), (), s32[]{:S(2)}) async-start(), calls=%async_computation.8 | async-start | bytes 9437184 | tf_op jit(solution)/shard_map/all_gather | solution.py:39
  68.3 135.3 %copy-start.9 = (f32[4096,64]{0,1:T(8,128)S(1)}, f32[4096,64]{0,1:T(8,128)}, u32[]{:S(2)}) copy-start(f32[4096,64]{0,1:T(8,128)} %param.6) | copy-start | bytes 3145732
  68.3 179.2 %all-reduce.11.cloned.1.call-start = ((), (), s32[]{:S(2)}) async-start(), calls=%async_computation.1 | async-start | bytes 2097152 | tf_op jit(solution)/shard_map/psum | solution.py:36
  213.0 170.1 %all-gather.19.cloned.1.call-start = ((), (), s32[]{:S(2)}) async-start(), calls=%async_computation.9 | async-start | bytes 9437184 | tf_op jit(solution)/shard_map/all_gather | solution.py:39
  257.9 179.2 %all-reduce.13.cloned.1.call-start = ((), (), s32[]{:S(2)}) async-start(), calls=%async_computation.2 | async-start | bytes 2097152 | tf_op jit(solution)/shard_map/psum | solution.py:36
  402.5 170.1 %all-gather.21.cloned.1.call-start = ((), (), s32[]{:S(2)}) async-start(), calls=%async_computation.10 | async-start | bytes 9437184 | tf_op jit(solution)/shard_map/all_gather | solution.py:39
  447.5 179.2 %all-reduce.15.cloned.1.call-start = ((), (), s32[]{:S(2)}) async-start(), calls=%async_computation.3 | async-start | bytes 2097152 | tf_op jit(solution)/shard_map/psum | solution.py:36
  592.1 170.1 %all-gather.23.cloned.1.call-start = ((), (), s32[]{:S(2)}) async-start(), calls=%async_computation.11 | async-start | bytes 9437184 | tf_op jit(solution)/shard_map/all_gather | solution.py:39
  637.1 180.3 %all-reduce.17.cloned.1.call-start = ((), (), s32[]{:S(2)}) async-start(), calls=%async_computation.4 | async-start | bytes 2097152 | tf_op jit(solution)/shard_map/psum | solution.py:36
  772.5 1.1 copy-start
  782.8 170.0 %all-gather.25.cloned.1.call-start = ((), (), s32[]{:S(2)}) async-start(), calls=%async_computation.12 | async-start | bytes 9437184 | tf_op jit(solution)/shard_map/all_gather | solution.py:39
  827.7 180.3 %all-reduce.19.cloned.1.call-start = ((), (), s32[]{:S(2)}) async-start(), calls=%async_computation.5 | async-start | bytes 2097152 | tf_op jit(solution)/shard_map/psum | solution.py:36
  952.8 10.2 copy-start.1
  963.2 1.0 copy-start.3
  973.4 170.0 %all-gather.27.cloned.1.call-start = ((), (), s32[]{:S(2)}) async-start(), calls=%async_computation.13 | async-start | bytes 9437184 | tf_op jit(solution)/shard_map/all_gather | solution.py:39
  1018.2 180.3 %all-reduce.21.cloned.1.call-start = ((), (), s32[]{:S(2)}) async-start(), calls=%async_computation.6 | async-start | bytes 2097152 | tf_op jit(solution)/shard_map/psum | solution.py:36
  1143.3 10.3 copy-start.2
  1143.3 10.3 copy-start.4
  1153.8 1.0 copy-start.6
  1163.9 170.0 %all-gather.29.cloned.1.call-start = ((), (), s32[]{:S(2)}) async-start(), calls=%async_computation.14 | async-start | bytes 9437184 | tf_op jit(solution)/shard_map/all_gather | solution.py:39
  1208.8 180.3 %all-reduce.23.cloned.1.call-start = ((), (), s32[]{:S(2)}) async-start(), calls=%async_computation.7 | async-start | bytes 2097152 | tf_op jit(solution)/shard_map/psum | solution.py:36
  1333.9 10.3 copy-start.5
  1333.9 10.3 copy-start.7
  1344.4 1.0 copy-start.8
  1354.5 170.0 %all-gather.31.cloned.1.call-start = ((), (), s32[]{:S(2)}) async-start(), calls=%async_computation.15 | async-start | bytes 9437184 | tf_op jit(solution)/shard_map/all_gather | solution.py:39
  1399.4 181.8 %copy-start.11 = (f32[9]{0:T(128)S(1)}, f32[9]{0:T(128)}, u32[]{:S(2)}) copy-start(f32[9]{0:T(128)} %constant.23.clone) | copy-start | bytes 112
Sparse Core Ops, SparseCore 0:
  18.9 39.0 all-reduce.8
  68.5 124.9 all-gather.16
  213.1 34.4 all-reduce.10
  258.1 124.9 all-gather.18
  402.7 34.4 all-reduce.12
  447.6 124.9 all-gather.20
  592.3 34.4 all-reduce.14
  637.2 124.9 all-gather.22
  782.9 34.4 all-reduce.16
  827.8 124.9 all-gather.24
  973.5 34.4 all-reduce.18
  1018.4 124.9 all-gather.26
  1164.1 34.4 all-reduce.20
  1208.9 124.9 all-gather.28
  1354.6 34.4 all-reduce.22
  1399.6 124.9 all-gather.30
